TPU v7x, 512 devices: a whole 4x4x16 slice. The times are simulated.
512 devices in a mesh: dp: 8 (over z_hi, x), row: 8 (over y, core), col: 8 (over z_lo).
Axes of the slice: x: 4, y: 4, z: 16 (z_hi: 2, z_lo: 8; z = z_hi * 8 + z_lo), core: 2. Of those that a mesh axis runs over, the one named last changes fastest.
Arguments:
- tokens: bfloat16 [65536, 8192], P(('dp', 'row', 'col')), parts along dimension 0, may hold values from -60 to 60
- norm_gain: float32 [8192], replicated, may hold values from 0.1 to 1.9
- w_key: bfloat16 [8192, 1024], P('row', 'col'), may hold values from -0.0625 to 0.0625
- w_value: bfloat16 [8192, 1024], P('row', 'col'), may hold values from -0.0625 to 0.0625
Outputs:
- key_rows: bfloat16 [65536, 1024], P(('dp', 'row', 'col')), parts along dimension 0
- value_rows: bfloat16 [65536, 1024], P(('dp', 'row', 'col')), parts along dimension 0
There are 8 independent parts, one for each index of `dp`. A program takes and returns all parts, laid end to end along the dimension named above; an argument that names none is the same for every part. Nothing has to cross between parts.
All inputs are finite; a program needn't handle non-finite values.
Results may differ from a plain program's by a relative error of at most 0.014.
Values may be sent and summed in bfloat16 or wider, within the bound.
A program may use at most 64 MiB of HBM per device.

v0:
```python
import jax
import jax.numpy as jnp
from jax import lax
from jax.sharding import PartitionSpec as P

HEAD = 128
rope_base = 500000.0


def rotate(projected, positions):
    row_count = projected.shape[0]
    head_count = projected.shape[1] // HEAD
    half_head = HEAD // 2
    frequency = rope_base ** (-2.0 * jnp.arange(half_head, dtype=jnp.float32) / HEAD)
    angles = positions.astype(jnp.float32)[:, None] * frequency[None, :]
    cosine = jnp.cos(angles)[:, None, :]
    sine = jnp.sin(angles)[:, None, :]
    split_heads = projected.reshape(row_count, head_count, HEAD)
    first = split_heads[:, :, :half_head]
    second = split_heads[:, :, half_head:]
    turned = jnp.concatenate(
        [first * cosine - second * sine, second * cosine + first * sine], axis=2
    )
    return turned.reshape(row_count, head_count * HEAD)


def body(tokens, norm_gain, w_key, w_value):
    col_count = lax.axis_size("col")
    row_index = lax.axis_index("row")
    col_index = lax.axis_index("col")
    own_rows = tokens.shape[0]
    widened = tokens.astype(jnp.float32)
    inverse_rms = lax.rsqrt(jnp.mean(widened * widened, axis=1, keepdims=True) + 1e-05)
    normed = (widened * inverse_rms * norm_gain[None, :]).astype(jnp.bfloat16)
    tile = lax.all_to_all(normed, "row", split_axis=1, concat_axis=0, tiled=True)
    key_weights, value_weights = (
        lax.all_gather(w_key, "col", axis=1, tiled=True),
        lax.all_gather(w_value, "col", axis=1, tiled=True),
    )
    key_part = jnp.dot(tile, key_weights, preferred_element_type=jnp.float32)
    value_part = jnp.dot(tile, value_weights, preferred_element_type=jnp.float32)
    key_sum, value_sum = (
        lax.psum_scatter(
            key_part.astype(jnp.bfloat16), "row", scatter_dimension=0, tiled=True
        ).astype(jnp.float32),
        lax.psum_scatter(
            value_part.astype(jnp.bfloat16), "row", scatter_dimension=0, tiled=True
        ).astype(jnp.float32),
    )
    positions = (row_index * col_count + col_index) * own_rows + jnp.arange(
        own_rows, dtype=jnp.int32
    )
    key_rows = rotate(key_sum, positions).astype(jnp.bfloat16)
    value_rows = value_sum.astype(jnp.bfloat16)
    return (key_rows, value_rows)


def solution(mesh):
    placed = (P(("dp", "row", "col"), None), P(), P("row", "col"), P("row", "col"))
    return jax.shard_map(
        body,
        mesh=mesh,
        in_specs=placed,
        out_specs=(P(("dp", "row", "col"), None), P(("dp", "row", "col"), None)),
        check_vma=False,
    )
```

profile of v0, /device:TPU:2, one launch (start us, length us, event | category | flops | bytes accessed | tf_op | source)
XLA Modules:
  0.0 248.9 jit_solution(14497560311085529130)
XLA Ops:
  7.2 0.0 all-gather.3.cloned.1.call-start
  7.2 0.7 all-gather.3.cloned.1.call-update
  7.9 0.0 all-gather.5.cloned.1.call-start
  7.9 0.7 all-gather.5.cloned.1.call-update
  8.6 0.0 reduce-scatter.3.cloned.1.call-start
  8.7 3.2 %copy.6 = bf16[128,8192]{0,1:T(8,128)(2,1)S(1)} copy(bf16[128,8192]{1,0:T(8,128)(2,1)} %param.4) | data formatting | bytes 4194304 | tf_op args[0]
  11.9 1.1 fusion
  13.0 3.5 %fusion.2 = bf16[128,8192]{0,1:T(8,128)(2,1)S(1)} fusion(bf16[128,8192]{0,1:T(8,128)(2,1)S(1)} %copy.6, f32[8192]{0:T(1024)S(1)} %copy-done.1, f32[128]{0:T(128)S(1)} %add_rsqrt_fusion), kind=kLoop, calls=%fused_computation.4 | loop fusion | flops 4194304 | bytes 4227584 | tf_op jit(solution)/shard_map/convert_element_type | solution.py:34
  16.5 31.8 %all_to_all.19 = bf16[128,8,1024]{0,2,1:T(8,128)(2,1)S(1)} all-to-all(bf16[128,8,1024]{0,2,1:T(8,128)(2,1)S(1)} %bitcast.14), channel_id=1, replica_groups=mesh['dp'=8,'row'=8,'col'=8] {'row'}, dimensions={1} | all-to-all | bytes 4194304 | tf_op jit(solution)/shard_map/all_to_all | solution.py:35
  48.3 2.6 %copy.7 = bf16[8,128,1024]{2,1,0:T(8,128)(2,1)} copy(bf16[8,128,1024]{1,2,0:T(8,128)(2,1)S(1)} %bitcast.15) | data formatting | bytes 4194304 | tf_op jit(solution)/shard_map/all_to_all | solution.py:35
  50.9 37.4 %all-gather.3.cloned.1.call-done = bf16[1024,1024]{1,0:T(8,128)(2,1)} async-done(((bf16[1024,128]{1,0:T(8,128)(2,1)}), bf16[1024,1024]{1,0:T(8,128)(2,1)}) %all-gather.3.cloned.1.call-update) | async-done | bytes 2097168 | tf_op jit(solution)/shard_map/all_gather | solution.py:37
  88.3 5.9 %convolution_convert_fusion.1 = bf16[1024,1024]{1,0:T(8,128)(2,1)} fusion(bf16[1024,1024]{1,0:T(8,128)(2,1)} %bitcast.17, bf16[1024,1024]{1,0:T(8,128)(2,1)} %all-gather.3.cloned.1.call-done), kind=kOutput, calls=%fused_computation.6 | convolution fusion | flops 2148532224 | bytes 6291456 | tf_op jit(solution)/shard_map/dot_general | solution.py:40
  94.2 0.0 reduce-scatter.3.cloned.1.call-update
  94.2 0.0 reduce-scatter.5.cloned.1.call-start
  94.3 65.2 %all-gather.5.cloned.1.call-done = bf16[1024,1024]{1,0:T(8,128)(2,1)} async-done(((bf16[1024,128]{1,0:T(8,128)(2,1)}), bf16[1024,1024]{1,0:T(8,128)(2,1)}) %all-gather.5.cloned.1.call-update) | async-done | bytes 2097168 | tf_op jit(solution)/shard_map/all_gather | solution.py:38
  159.5 5.3 %convolution_convert_fusion = bf16[1024,1024]{1,0:T(8,128)(2,1)} fusion(bf16[1024,1024]{1,0:T(8,128)(2,1)S(1)} %bitcast.18, bf16[1024,1024]{1,0:T(8,128)(2,1)} %all-gather.5.cloned.1.call-done), kind=kOutput, calls=%fused_computation.5 | convolution fusion | flops 2148532224 | bytes 6291456 | tf_op jit(solution)/shard_map/dot_general | solution.py:41
  164.8 0.3 multiply_cosine_fusion
  165.1 33.8 %reduce-scatter.3.cloned.1.call-done = bf16[128,1024]{1,0:T(8,128)(2,1)} async-done(((bf16[1024,1024]{1,0:T(8,128)(2,1)}), bf16[128,1024]{1,0:T(8,128)(2,1)}) %reduce-scatter.3.cloned.1.call-update) | async-done | bytes 262160 | tf_op jit(solution)/shard_map/reduce_scatter | solution.py:43
  198.9 1.0 convert_bitcast_fusion
  199.9 0.1 copy.8
  200.0 0.3 subtract_convert_fusion
  200.3 0.1 pad_maximum_fusion
  200.4 0.8 copy.11
  201.2 41.2 %reduce-scatter.5.cloned.1.call-done = bf16[128,1024]{1,0:T(8,128)(2,1)} async-done(((bf16[1024,1024]{1,0:T(8,128)(2,1)}), bf16[128,1024]{1,0:T(8,128)(2,1)}) %reduce-scatter.5.cloned.1.call-update) | async-done | bytes 262160 | tf_op jit(solution)/shard_map/reduce_scatter | solution.py:46
  (8 shorter events, 0.1 us)
Async XLA Ops:
  7.2 81.2 %all-gather.3.cloned.1.call-start = ((), (), s32[]{:S(2)}) async-start(), calls=%async_computation.3 | async-start | bytes 2359296 | tf_op jit(solution)/shard_map/all_gather | solution.py:37
  7.9 151.6 %all-gather.5.cloned.1.call-start = ((), (), s32[]{:S(2)}) async-start(), calls=%async_computation.5 | async-start | bytes 2359296 | tf_op jit(solution)/shard_map/all_gather | solution.py:38
  8.6 190.2 %reduce-scatter.3.cloned.1.call-start = ((), (), s32[]{:S(2)}) async-start(), calls=%async_computation.4 | async-start | bytes 2359296 | tf_op jit(solution)/shard_map/reduce_scatter | solution.py:43
  11.9 1.1 copy-start.1
  94.2 65.3 %copy-start = (bf16[8,128,1024]{2,1,0:T(8,128)(2,1)S(1)}, bf16[8,128,1024]{2,1,0:T(8,128)(2,1)}, u32[]{:S(2)}) copy-start(bf16[8,128,1024]{2,1,0:T(8,128)(2,1)} %copy.7) | copy-start | bytes 6291460
  94.2 148.2 %reduce-scatter.5.cloned.1.call-start = ((), (), s32[]{:S(2)}) async-start(), calls=%async_computation.6 | async-start | bytes 2359296 | tf_op jit(solution)/shard_map/reduce_scatter | solution.py:46
Sparse Core Ops, SparseCore 0:
  10.0 78.2 all-gather.2
  90.3 69.0 all-gather.4
  162.3 36.5 reduce-scatter.2
  202.2 40.1 reduce-scatter.4
where the time goes:
time: 249 us
  waiting for transfers between devices  179 us (72%)
  blocking collectives  31.8 us (13%)
  between operations  13.8 us (6%)
  matrix products  11.1 us (4%)
  local copies, waits for them, and re-layouts  6.71 us (3%)
  other arithmetic  6.31 us (3%)
    all_gather x1, waiting for transfers between devices, body(): lax.all_gather(w_value, 'col', axis=1, tiled=True)  65.2 us
    reduce_scatter x1, waiting for transfers between devices, body(): lax.psum_scatter(value_part.astype(jnp.bfloat16), 'row', scatter_dimensio...  41.2 us
    all_gather x1, waiting for transfers between devices, body(): lax.all_gather(w_key, 'col', axis=1, tiled=True)  37.4 us
    reduce_scatter x1, waiting for transfers between devices, body(): lax.psum_scatter(key_part.astype(jnp.bfloat16), 'row', scatter_dimension=...  33.8 us
    all_to_all x1, blocking collectives, body(): lax.all_to_all(normed, 'row', split_axis=1, concat_axis=0, tiled=True)  31.8 us
    dot_general x1, matrix products, body(): key_part = jnp.dot(tile, key_weights, preferred_element_type=jnp.float32)  5.86 us
    dot_general x1, matrix products, body(): jnp.dot(tile, value_weights, preferred_element_type=jnp.float32)  5.26 us
  transfers between devices with their start and end apart: 4, of which 4 were waited for; matrix products, arithmetic and copies ran while one was open for 10% of the time, Pallas kernels for 0%

commit v1 on v0

--- a/solution.py
+++ b/solution.py
@@ -35,7 +35,9 @@
     tile = lax.all_to_all(normed, "row", split_axis=1, concat_axis=0, tiled=True)
     key_weights, value_weights = (
         lax.all_gather(w_key, "col", axis=1, tiled=True),
-        lax.all_gather(w_value, "col", axis=1, tiled=True),
+        jnp.concatenate(
+            lax.all_to_all(jnp.stack([w_value] * lax.axis_size("col")), "col", 0, 0), axis=1
+        ),
     )
     key_part = jnp.dot(tile, key_weights, preferred_element_type=jnp.float32)
     value_part = jnp.dot(tile, value_weights, preferred_element_type=jnp.float32)

time: 249 us -> 279 us (1.12)
  waiting for transfers between devices: 179 us -> 221 us
  blocking collectives: 31.8 us -> 0 us
  starting transfers between devices: 0.16 us -> 17.2 us
    all_gather x1 -> x0, waiting for transfers between devices: 65.2 us -> none  [body(): lax.all_gather(w_value, 'col', axis=1, tiled=True)]
    all_gather x1, waiting for transfers between devices: 37.4 us -> 93.5 us  [body(): lax.all_gather(w_key, 'col', axis=1, tiled=True)]
    all_to_all x0 -> x2, waiting for transfers between devices: none -> 44.5 us  [the longest x1 26.3 us: body(): lax.all_to_all(normed, 'row', split_axis=1, concat_axis=0, tiled=True)]
    all_to_all x1 -> x0, blocking collectives: 31.8 us -> none  [body(): lax.all_to_all(normed, 'row', split_axis=1, concat_axis=0, tiled=True)]
    all_to_all x0 -> x2, starting transfers between devices: none -> 17.1 us  [the longest x1 12.5 us: body(): lax.all_to_all(jnp.stack([w_value] * lax.axis_size('col')), 'col', 0, 0)]
    reduce_scatter x1, waiting for transfers between devices: 33.8 us -> 41.1 us  [body(): lax.psum_scatter(key_part.astype(jnp.bfloat16), 'row', scatter_dimension=...]
  transfers between devices with their start and end apart: 4 -> 5, of which waited for: 4 -> 5; matrix products, arithmetic and copies ran while one was open for 10% -> 7% of each run, Pallas kernels for 0% -> 0%
where the time goes in v1:
time: 279 us
  waiting for transfers between devices  221 us (79%)
  starting transfers between devices  17.2 us (6%)
  between operations  13.8 us (5%)
  matrix products  11.2 us (4%)
  local copies, waits for them, and re-layouts  8.5 us (3%)
  other arithmetic  7.17 us (3%)
    all_gather x1, waiting for transfers between devices, body(): lax.all_gather(w_key, 'col', axis=1, tiled=True)  93.5 us
    reduce_scatter x1, waiting for transfers between devices, body(): lax.psum_scatter(value_part.astype(jnp.bfloat16), 'row', scatter_dimensio...  41.4 us
    reduce_scatter x1, waiting for transfers between devices, body(): lax.psum_scatter(key_part.astype(jnp.bfloat16), 'row', scatter_dimension=...  41.1 us
    all_to_all x1, waiting for transfers between devices, body(): lax.all_to_all(normed, 'row', split_axis=1, concat_axis=0, tiled=True)  26.3 us
    all_to_all x1, waiting for transfers between devices, body(): lax.all_to_all(jnp.stack([w_value] * lax.axis_size('col')), 'col', 0, 0)  18.2 us
    all_to_all x1, starting transfers between devices, body(): lax.all_to_all(jnp.stack([w_value] * lax.axis_size('col')), 'col', 0, 0)  12.5 us
    dot_general x1, matrix products, body(): key_part = jnp.dot(tile, key_weights, preferred_element_type=jnp.float32)  5.87 us
  transfers between devices with their start and end apart: 5, of which 5 were waited for; matrix products, arithmetic and copies ran while one was open for 7% of the time, Pallas kernels for 0%

profile of v1, /device:TPU:2, one launch (start us, length us, event | category | flops | bytes accessed | tf_op | source)
XLA Modules:
  0.0 279.1 jit_solution(5175636371358946661)
XLA Ops:
  7.2 3.2 %copy.7 = bf16[128,8192]{0,1:T(8,128)(2,1)S(1)} copy(bf16[128,8192]{1,0:T(8,128)(2,1)} %param.4) | data formatting | bytes 4194304 | tf_op args[0]
  10.4 1.1 fusion
  11.5 4.3 %fusion.2 = bf16[128,8192]{0,1:T(8,128)(2,1)} fusion(bf16[128,8192]{0,1:T(8,128)(2,1)S(1)} %copy.7, f32[8192]{0:T(1024)S(1)} %copy-done.2, f32[128]{0:T(128)S(1)} %add_rsqrt_fusion), kind=kLoop, calls=%fused_computation.4 | loop fusion | flops 4194304 | bytes 4227584 | tf_op jit(solution)/shard_map/convert_element_type | solution.py:34
  15.9 4.6 %all-to-all-start = ((bf16[128,8,1024]{0,2,1:T(8,128)(2,1)}), bf16[128,8,1024]{0,2,1:T(8,128)(2,1)S(1)}, u32[]{:S(2)}, u32[]{:S(2)}) async-start(bf16[128,8,1024]{0,2,1:T(8,128)(2,1)} %bitcast.18), calls=%async_computation | async-start | bytes 4194304 | tf_op jit(solution)/shard_map/all_to_all | solution.py:35
  20.5 0.7 all-gather.2.cloned.1.call-update
  21.2 0.1 copy.9
  21.4 26.3 %all-to-all-done = bf16[128,8,1024]{0,2,1:T(8,128)(2,1)S(1)} async-done(((bf16[128,8,1024]{0,2,1:T(8,128)(2,1)}), bf16[128,8,1024]{0,2,1:T(8,128)(2,1)S(1)}, u32[]{:S(2)}, u32[]{:S(2)}) %all-to-all-start) | async-done | bytes 2097184 | tf_op jit(solution)/shard_map/all_to_all | solution.py:35
  47.7 1.6 stack.2
  49.3 12.5 %all-to-all-start.1 = ((bf16[8,1024,128]{1,2,0:T(8,128)(2,1)}), bf16[8,1024,128]{1,2,0:T(8,128)(2,1)}, u32[]{:S(2)}, u32[]{:S(2)}) async-start(bf16[8,1024,128]{1,2,0:T(8,128)(2,1)} %stack.2), calls=%async_computation.2 | async-start | bytes 4194304 | tf_op jit(solution)/shard_map/all_to_all | solution.py:39
  61.8 0.0 reduce-scatter.3.cloned.1.call-start
  61.9 2.7 copy.8
  64.5 93.5 %all-gather.2.cloned.1.call-done = bf16[1024,1024]{1,0:T(8,128)(2,1)} async-done(((bf16[1024,128]{1,0:T(8,128)(2,1)}), bf16[1024,1024]{1,0:T(8,128)(2,1)}) %all-gather.2.cloned.1.call-update) | async-done | bytes 2097168 | tf_op jit(solution)/shard_map/all_gather | solution.py:37
  158.0 5.9 %convolution_convert_fusion.1 = bf16[1024,1024]{1,0:T(8,128)(2,1)} fusion(bf16[1024,1024]{1,0:T(8,128)(2,1)} %bitcast.20, bf16[1024,1024]{1,0:T(8,128)(2,1)} %all-gather.2.cloned.1.call-done), kind=kOutput, calls=%fused_computation.6 | convolution fusion | flops 2148532224 | bytes 6291456 | tf_op jit(solution)/shard_map/dot_general | solution.py:42
  163.9 0.0 reduce-scatter.5.cloned.1.call-start
  164.0 18.2 %all-to-all-done.1 = bf16[8,1024,128]{1,2,0:T(8,128)(2,1)} async-done(((bf16[8,1024,128]{1,2,0:T(8,128)(2,1)}), bf16[8,1024,128]{1,2,0:T(8,128)(2,1)}, u32[]{:S(2)}, u32[]{:S(2)}) %all-to-all-start.1) | async-done | bytes 2097184 | tf_op jit(solution)/shard_map/all_to_all | solution.py:39
  182.1 5.3 %convolution_convert_fusion = bf16[1024,1024]{1,0:T(8,128)(2,1)} fusion(bf16[1024,1024]{1,0:T(8,128)(2,1)S(1)} %bitcast.21, bf16[1024,1024]{0,1:T(8,128)(2,1)} %bitcast.4), kind=kOutput, calls=%fused_computation.5 | convolution fusion | flops 2148532224 | bytes 6291456 | tf_op jit(solution)/shard_map/dot_general | solution.py:43
  187.5 0.3 multiply_cosine_fusion
  187.8 41.1 %reduce-scatter.3.cloned.1.call-done = bf16[128,1024]{1,0:T(8,128)(2,1)} async-done(((bf16[1024,1024]{1,0:T(8,128)(2,1)}), bf16[128,1024]{1,0:T(8,128)(2,1)}) %reduce-scatter.3.cloned.1.call-update) | async-done | bytes 262160 | tf_op jit(solution)/shard_map/reduce_scatter | solution.py:45
  228.9 1.0 convert_bitcast_fusion
  229.9 0.1 copy.10
  230.0 0.3 subtract_convert_fusion
  230.2 0.1 pad_maximum_fusion
  230.4 0.8 copy.13
  231.2 41.4 %reduce-scatter.5.cloned.1.call-done = bf16[128,1024]{1,0:T(8,128)(2,1)} async-done(((bf16[1024,1024]{1,0:T(8,128)(2,1)}), bf16[128,1024]{1,0:T(8,128)(2,1)}) %reduce-scatter.5.cloned.1.call-update) | async-done | bytes 262160 | tf_op jit(solution)/shard_map/reduce_scatter | solution.py:48
  (12 shorter events, 0.1 us)
Async XLA Ops:
  10.4 1.1 copy-start.2
  15.9 5.3 %copy-start.1 = (bf16[1024,128]{1,0:T(8,128)(2,1)S(1)}, bf16[1024,128]{1,0:T(8,128)(2,1)}, u32[]{:S(2)}) copy-start(bf16[1024,128]{1,0:T(8,128)(2,1)} %param.7) | copy-start | bytes 786436
  15.9 31.8 %all-to-all-start = ((bf16[128,8,1024]{0,2,1:T(8,128)(2,1)}), bf16[128,8,1024]{0,2,1:T(8,128)(2,1)S(1)}, u32[]{:S(2)}, u32[]{:S(2)}) async-start(bf16[128,8,1024]{0,2,1:T(8,128)(2,1)} %bitcast.18), calls=%async_computation | async-start | bytes 4194304 | tf_op jit(solution)/shard_map/all_to_all | solution.py:35
  20.5 137.5 %all-gather.2.cloned.1.call-start = ((), (), s32[]{:S(2)}) async-start(), calls=%async_computation.4 | async-start | bytes 2359296 | tf_op jit(solution)/shard_map/all_gather | solution.py:37
  49.3 132.9 %all-to-all-start.1 = ((bf16[8,1024,128]{1,2,0:T(8,128)(2,1)}), bf16[8,1024,128]{1,2,0:T(8,128)(2,1)}, u32[]{:S(2)}, u32[]{:S(2)}) async-start(bf16[8,1024,128]{1,2,0:T(8,128)(2,1)} %stack.2), calls=%async_computation.2 | async-start | bytes 4194304 | tf_op jit(solution)/shard_map/all_to_all | solution.py:39
  61.8 167.1 %reduce-scatter.3.cloned.1.call-start = ((), (), s32[]{:S(2)}) async-start(), calls=%async_computation.5 | async-start | bytes 2359296 | tf_op jit(solution)/shard_map/reduce_scatter | solution.py:45
  163.9 18.3 %copy-start = (bf16[8,128,1024]{2,1,0:T(8,128)(2,1)S(1)}, bf16[8,128,1024]{2,1,0:T(8,128)(2,1)}, u32[]{:S(2)}) copy-start(bf16[8,128,1024]{2,1,0:T(8,128)(2,1)} %copy.8) | copy-start | bytes 6291460
  163.9 108.7 %reduce-scatter.5.cloned.1.call-start = ((), (), s32[]{:S(2)}) async-start(), calls=%async_computation.6 | async-start | bytes 2359296 | tf_op jit(solution)/shard_map/reduce_scatter | solution.py:48
Sparse Core Ops, SparseCore 0:
  23.3 134.6 all-gather.1
  164.0 64.7 reduce-scatter.2
  232.3 40.2 reduce-scatter.4
